TPU v7x, 32 devices: a whole 2x2x4 slice. The times are simulated.
32 devices in a mesh: grp: 2 (over y), row: 4 (over z), col: 2 (over x), sub: 2 (over core).
Axes of the slice: x: 2, y: 2, z: 4, core: 2. Of those that a mesh axis runs over, the one named last changes fastest.
Arguments:
- recordings: float32 [4, 4096, 2000], P('grp', ('row', 'col'), 'sub'), parts along dimension 0, may hold values from -640 to 640
- filter_taps: float32 [129], replicated, may hold values from -0.5 to 0.5
- slot_table: int32 [4, 1024], P('row'), may hold values from 0 to 1023, each once within a row
- lag_count: int32 [4096], replicated, may hold values from 1 to 17
Outputs:
- xcorr: bfloat16 [34, 4096, 2, 2048], P('grp', ('row', 'sub'), 'col'), parts along dimension 0
There are 2 independent parts, one for each index of `grp`. A program takes and returns all parts, laid end to end along the dimension named above; an argument that names none is the same for every part. Nothing has to cross between parts.
Inputs may be any that keep to these rules, and one draw needn't show every extreme that they name: Each row of slot_table names every slot of the block exactly once.
All inputs are finite; a program needn't handle non-finite values.
Results may differ from a plain program's by a relative error of at most 0.0052.
Values may be sent and summed in bfloat16 or wider, within the bound.
A program may use at most 192 MiB of HBM per device.

v0:
```python
import math

import jax
import jax.numpy as jnp
from jax import lax
from jax.sharding import PartitionSpec as P

LAGS = 17


stability = 1e-05


def padded_2(block, sides, width):
    for axis, dim in sides:
        count = lax.axis_size(axis)
        forward = [(i, i + 1) for i in range(count - 1)]
        backward = [(target, source) for source, target in forward]
        low = lax.ppermute(
            lax.slice_in_dim(block, block.shape[dim] - width, None, axis=dim), axis, forward
        )
        high = lax.ppermute(lax.slice_in_dim(block, 0, width, axis=dim), axis, backward)
        block = jnp.concatenate([low, block, high], axis=dim)
    return block


def correlate(row_data, column_data, lag_limits, factor, lag_total):
    samples = column_data.shape[2]
    padded_cols = jnp.pad(column_data, ((0, 0), (0, 0), (0, lag_total)))

    def single_lag(lag_index):
        shifted = lax.dynamic_slice_in_dim(padded_cols, lag_index, samples, 2)
        product = jnp.einsum("sat,sbt->ab", row_data, shifted, preferred_element_type=jnp.float32)
        return jnp.where(lag_index < lag_limits[None, :], product * factor, 0.0).astype(
            jnp.bfloat16
        )

    return lax.map(single_lag, jnp.arange(lag_total, dtype=jnp.int32))


def shards(recordings, filter_taps, slot_table, lag_count):
    margin = (filter_taps.shape[0] - 1) // 2
    padded = padded_2(recordings, (("sub", 2),), margin)
    segments, channels, extent = padded.shape
    filtered = lax.conv_general_dilated(
        padded.reshape(segments * channels, 1, extent),
        filter_taps.reshape(1, 1, -1),
        (2,),
        "VALID",
        precision=lax.Precision.HIGHEST,
    ).reshape(segments, channels, -1)
    energy = lax.psum(jnp.sum(filtered * filtered, axis=2), "sub")
    length = filtered.shape[2] * lax.axis_size("sub")
    whitened = (filtered * lax.rsqrt(energy[:, :, None] / length + stability)).astype(jnp.bfloat16)
    whole = lax.all_gather(whitened, "sub", axis=2, tiled=True)
    block_rows = lax.all_gather(whole, "col", axis=1, tiled=True)
    portion = block_rows.shape[1] // lax.axis_size("sub")
    chosen = lax.dynamic_slice_in_dim(slot_table[0], lax.axis_index("sub") * portion, portion)
    row_data = jnp.take(block_rows, chosen, axis=1)
    row_count = lax.axis_size("row")
    col_count = lax.axis_size("col")
    lag_limits = lax.dynamic_slice_in_dim(
        lag_count.reshape(row_count, col_count * channels),
        lax.axis_index("col") * channels,
        channels,
        1,
    ).reshape(-1)
    factor = 1.0 / math.sqrt(segments * length)
    segment_cols = lax.all_gather(whole, "row", axis=1, tiled=True)
    limits_here = lax.slice_in_dim(lag_limits, 0, segment_cols.shape[1], axis=0)
    result = correlate(row_data, segment_cols, limits_here, factor, LAGS)
    return result.reshape(LAGS, portion, 1, -1)


def solution(mesh):
    return jax.shard_map(
        shards,
        mesh=mesh,
        in_specs=(P("grp", ("row", "col"), "sub"), P(), P("row", None), P()),
        out_specs=P("grp", ("row", "sub"), "col", None),
        check_vma=False,
    )
```

profile of v0, /device:TPU:0, one launch (start us, length us, event | category | flops | bytes accessed | tf_op | source)
XLA Modules:
  0.0 1721.2 jit_solution(6695771380440782216)
XLA Ops:
  35.2 1143.3 %multiply_reduce_fusion = (f32[1024]{0:T(1024)S(1)}, f32[1024,500]{0,1:T(8,128)}) fusion(f32[1024,1,1128]{0,1,2:T(1,128)} %reshape.65, f32[1,1,129]{1,0,2:T(1,128)S(1)} %copy.22), kind=kOutput, calls=%fused_computation.14 | convolution fusion | flops 793598976 | bytes 6672900 | tf_op jit(solution)/shard_map/conv_general_dilated | solution.py:45
  1185.8 12.7 all-gather.4.cloned.1.call-done
  1202.5 56.1 %all-gather.8.cloned.1.call-done = bf16[2,1024,1000]{1,2,0:T(8,128)(2,1)} async-done(((bf16[2,512,1000]{1,2,0:T(8,128)(2,1)}), bf16[2,1024,1000]{1,2,0:T(8,128)(2,1)}) %all-gather.8.cloned.1.call-update) | async-done | bytes 4096016 | tf_op jit(solution)/shard_map/all_gather | solution.py:56
  1258.6 11.5 copy.25
  1270.1 27.3 %gather_fusion = bf16[512,2,1000]{2,1,0:T(2,128)(2,1)S(1)} fusion(bf16[2,1024,1000]{2,0,1:T(2,128)(2,1)} %copy.25, s32[1024]{0:T(1024)S(1)} %pad_clamp_fusion), kind=kCustom, calls=%fused_computation | custom fusion | bytes 4098048 | tf_op jit(solution)/shard_map/jit(_take)/gather | solution.py:59
  1307.4 99.3 %all-gather.6.cloned.1.call-done = bf16[2,2048,1000]{1,2,0:T(8,128)(2,1)} async-done(((bf16[2,512,1000]{1,2,0:T(8,128)(2,1)}), bf16[2,2048,1000]{1,2,0:T(8,128)(2,1)}) %all-gather.6.cloned.1.call-update) | async-done | bytes 8192016 | tf_op jit(solution)/shard_map/all_gather | solution.py:69
  1414.9 299.4 %while.10 = (s32[]{:T(128)}, bf16[17,512,2048]{2,1,0:T(8,128)(2,1)}, s32[17]{0:T(128)S(1)}, s32[4,512]{1,0:T(4,128)S(1)}, bf16[2,2048,1017]{1,2,0:T(8,128)(2,1)}...) while((s32[]{:T(128)}, bf16[17,512,2048]{2,1,0:T(8,128)(2,1)}, s32[17]{0:T(128)S(1)}, ...), condition=%wide.region_3.4_spmd, body=%wide.region_2.3_spmd.sunk | while | flops 4197451776 | bytes 20742804 | solution.py:38
  1418.3 10.0 fusion.20
  1435.9 10.0 fusion.20
  1453.5 10.0 fusion.20
  1471.1 10.0 fusion.20
  1488.7 10.0 fusion.20
  1506.3 10.0 fusion.20
  1523.9 10.0 fusion.20
  1541.5 10.0 fusion.20
  1559.1 10.0 fusion.20
  1576.7 10.0 fusion.20
  1594.3 10.0 fusion.20
  1611.9 10.0 fusion.20
  1629.5 10.0 fusion.20
  1647.1 10.0 fusion.20
  1664.7 10.0 fusion.20
  1682.3 10.0 fusion.20
  1699.9 10.0 fusion.20
  (120 shorter events, 154.6 us)
Async XLA Ops:
  6.5 1191.9 %all-gather.4.cloned.1.call-start = ((), (), s32[]{:S(2)}) async-start(), calls=%async_computation | async-start | bytes 3072000 | tf_op jit(solution)/shard_map/all_gather | solution.py:55
  7.6 4.5 collective-permute-start
  10.0 3.4 collective-permute-start.1
  1185.7 16.7 copy-start
  1185.7 16.7 copy-start.1
  1185.7 72.9 %all-gather.8.cloned.1.call-start = ((), (), s32[]{:S(2)}) async-start(), calls=%async_computation.2 | async-start | bytes 6144000 | tf_op jit(solution)/shard_map/all_gather | solution.py:56
  1201.7 205.0 %all-gather.6.cloned.1.call-start = ((), (), s32[]{:S(2)}) async-start(), calls=%async_computation.1 | async-start | bytes 10240000 | tf_op jit(solution)/shard_map/all_gather | solution.py:69
Sparse Core Ops, SparseCore 0:
  1185.8 12.5 all-gather.3
  1201.8 56.7 all-gather.7
  1260.2 146.4 all-gather.5
where the time goes:
time: 1730 us; the launch traced here: 1720 us
  matrix products  1310 us (76%)
  waiting for transfers between devices  170 us (10%)
  local copies, waits for them, and re-layouts  166 us (10%)
  loops' own time  33.1 us (2%)
  other arithmetic  19.1 us (1%)
    conv_general_dilated x1, matrix products, shards(): lax.conv_general_dilated(padded.reshape(segments * channels, 1, extent),...  1140 us
    dot_general x17, matrix products, single_lag(): jnp.einsum('sat,sbt->ab', row_data, shifted, preferred_element_type=jnp.f...  170 us
    all_gather x1, waiting for transfers between devices, shards(): segment_cols = lax.all_gather(whole, 'row', axis=1, tiled=True)  99.3 us
    dynamic_update_slice x34, local copies, waits for them, and re-layouts, correlate(): return lax.map(single_lag, jnp.arange(lag_total, dtype=jnp.int32))  74.6 us
    all_gather x1, waiting for transfers between devices, shards(): block_rows = lax.all_gather(whole, 'col', axis=1, tiled=True)  56.1 us
  transfers between devices with their start and end apart: 5, of which 4 were waited for; matrix products, arithmetic and copies ran while one was open for 3% of the time, Pallas kernels for 0%

commit v1 on v0

v1 whole, which is shorter than its diff:
```python
import functools
import math

import jax
import jax.numpy as jnp
from jax import lax
from jax.experimental import pallas as pl
from jax.experimental.pallas import tpu as pltpu
from jax.sharding import PartitionSpec as P

LAGS = 17
PHASES = 8
SLOTS = 128
STABILITY = 1e-05


def nt_dot(a, b):
    return lax.dot_general(a, b, (((1,), (1,)), ((), ())), preferred_element_type=jnp.float32)


def nn_dot(a, b):
    return jnp.dot(a, b, preferred_element_type=jnp.float32)


def filter_kernel(samples, side_ref, own_ref, other_ref, taps_ref, out_ref, line, filtered):
    margin = 64
    width = own_ref.shape[1]
    window = 3 * 128
    order = lax.broadcasted_iota(jnp.int32, (128, window), 0)
    place = PHASES * (order % 16) + order // 16
    band = jnp.broadcast_to(taps_ref[...], (128, window))
    for bit in range(7):
        moved = pltpu.roll(band, 2 << bit, 1)
        band = jnp.where((place >> bit) & 1 == 1, moved, band)
    band_high = band.astype(jnp.bfloat16)
    band_low = (band - band_high.astype(jnp.float32)).astype(jnp.bfloat16)

    line[...] = jnp.zeros_like(line)

    @pl.when(side_ref[0] == 0)
    def _():
        line[margin : margin + width] = own_ref[0]
        line[margin + width : margin + 2 * width] = other_ref[0]

    @pl.when(side_ref[0] != 0)
    def _():
        line[margin : margin + width] = other_ref[0]
        line[margin + width : margin + 2 * width] = own_ref[0]

    tiles = SLOTS // 16
    row = lax.broadcasted_iota(jnp.int32, (128, 1), 0)
    energy = jnp.zeros((1, line.shape[1]), jnp.float32)
    for tile in range(tiles):
        part = line[256 * tile : 256 * tile + window]
        high = part.astype(jnp.bfloat16)
        low = (part - high.astype(jnp.float32)).astype(jnp.bfloat16)
        value = nn_dot(band_high, high) + (nn_dot(band_high, low) + nn_dot(band_low, high))
        index = PHASES * (16 * tile + row % 16) + row // 16
        value = jnp.where(index < samples, value, 0.0)
        energy = energy + jnp.sum(value * value, axis=0, keepdims=True)
        filtered[tile] = value
    scale = lax.rsqrt(energy / samples + STABILITY)
    for tile in range(tiles):
        value = (filtered[tile] * scale).astype(jnp.bfloat16)
        for phase in range(PHASES):
            out_ref[phase, 0, 16 * tile : 16 * tile + 16, :] = value[16 * phase : 16 * phase + 16]


def whiten(recordings, other, taps, side):
    segments, width, channels = recordings.shape
    half = channels // 2
    block = min(128, half)
    steps = half // block
    samples = width
    own_steps = steps
    if block % 128:
        recordings = lax.dynamic_slice_in_dim(recordings, side[0] * half, half, 2)
        own_steps = 0
    taps_row = jnp.pad(taps.reshape(1, -1), ((0, 0), (0, 384 - taps.shape[0])))
    out = pl.pallas_call(
        functools.partial(filter_kernel, samples),
        out_shape=jax.ShapeDtypeStruct((PHASES, segments, SLOTS, half), jnp.bfloat16),
        grid_spec=pltpu.PrefetchScalarGridSpec(
            num_scalar_prefetch=1,
            grid=(segments, steps),
            in_specs=[
                pl.BlockSpec((1, width, block), lambda s, c, side: (s, 0, side[0] * own_steps + c)),
                pl.BlockSpec((1, width, block), lambda s, c, side: (s, 0, c)),
                pl.BlockSpec((1, 384), lambda s, c, side: (0, 0)),
            ],
            out_specs=pl.BlockSpec((PHASES, 1, SLOTS, block), lambda s, c, side: (0, s, 0, c)),
            scratch_shapes=[
                pltpu.VMEM((256 * (SLOTS // 16 - 1) + 384, block), jnp.float32),
                pltpu.VMEM((SLOTS // 16, 128, block), jnp.float32),
            ],
        ),
        compiler_params=pltpu.CompilerParams(vmem_limit_bytes=16 << 20),
        name="whiten",
    )(side, recordings, other, taps_row)
    return out.reshape(PHASES * segments * SLOTS, half)


def rows_kernel(count, base_ref, slots_ref, *refs):
    pieces, out_ref = refs[:count], refs[count]
    phase = pl.program_id(0)
    rows = slots_ref.shape[0]
    total = None
    for k, piece in enumerate(pieces):
        width = piece.shape[1]
        channel = lax.broadcasted_iota(jnp.int32, (rows, width), 1) + base_ref[k]
        pick = (slots_ref[...] == channel).astype(jnp.float32).astype(jnp.bfloat16)
        term = nt_dot(pick, piece[...])
        total = term if total is None else total + term
    depth = total.shape[1]
    for carry in range(3):
        if carry:
            moved = jnp.concatenate(
                [
                    pltpu.roll(total[:, s : s + SLOTS], carry, 1)
                    for s in range(0, depth, SLOTS)
                ],
                axis=1,
            )
        else:
            moved = total
        start = pl.multiple_of((2 - carry) * PHASES * depth + phase * depth, depth)
        out_ref[:, pl.ds(start, depth)] = moved.astype(jnp.bfloat16)


def build_rows(slots, pieces, bases):
    rows = slots.shape[0]
    depth = pieces[0].shape[0] // PHASES
    return pl.pallas_call(
        functools.partial(rows_kernel, len(pieces)),
        out_shape=jax.ShapeDtypeStruct((rows, 3 * PHASES * depth), jnp.bfloat16),
        grid_spec=pltpu.PrefetchScalarGridSpec(
            num_scalar_prefetch=1,
            grid=(PHASES,),
            in_specs=[pl.BlockSpec((rows, 1), lambda j, base: (0, 0))]
            + [pl.BlockSpec((depth, p.shape[1]), lambda j, base: (j, 0)) for p in pieces],
            out_specs=pl.BlockSpec((rows, 3 * PHASES * depth), lambda j, base: (0, 0)),
        ),
        compiler_params=pltpu.CompilerParams(vmem_limit_bytes=24 << 20),
        name="rows",
    )(bases, slots, *pieces)


def correlate_kernel(factor, count, choices, depth, where_ref, rows_ref, limit_ref, *refs):
    pieces, out_ref, held, done = refs[: count * choices], refs[-3], refs[-2], refs[-1]
    lag = pl.program_id(0)
    length = PHASES * depth

    @pl.when(lag == 0)
    def _():
        for choice in range(choices):

            @pl.when(where_ref[3] == choice)
            def _():
                copies = [
                    pltpu.make_async_copy(pieces[count * choice + k], held.at[k], done.at[k])
                    for k in range(count)
                ]
                for copy in copies:
                    copy.start()
                for copy in copies:
                    copy.wait()

    start = pl.multiple_of((LAGS - 1 - lag) * depth, depth)
    rows = rows_ref[:, pl.ds(start, length)]
    width = held.shape[2]
    block = min(width, 256)
    for k in range(count):
        for first in range(0, width, block):
            spot = first
            if count > 1:
                spot = pl.multiple_of(where_ref[1 + k] * width + first, block)
            product = jnp.dot(
                rows, held[k, :, first : first + block], preferred_element_type=jnp.float32
            )
            keep = lag < limit_ref[:, pl.ds(spot, block)]
            out_ref[0, :, pl.ds(spot, block)] = jnp.where(keep, product * factor, 0.0).astype(
                jnp.bfloat16
            )


def correlate(rows, pieces, limits, where, factor, buffer):
    choices, count = len(pieces), len(pieces[0])
    depth = rows.shape[1] // (3 * PHASES)
    length = PHASES * depth
    portion = rows.shape[0]
    columns = limits.shape[1]
    run = pieces[0][0].shape[1]
    across = count * run
    pieces = [piece for group in pieces for piece in group]
    operands = [where, rows, limits, *pieces]
    in_specs = [
        pl.BlockSpec(rows.shape, lambda l, where: (0, 0), pipeline_mode=pl.Buffered(1)),
        pl.BlockSpec((1, across), lambda l, where: (0, where[0])),
    ] + [pl.BlockSpec(memory_space=pl.ANY) for _ in pieces]
    aliases = {}
    if buffer is not None:
        aliases = {len(operands): 0}
        operands.append(buffer)
        in_specs.append(pl.BlockSpec(memory_space=pl.ANY))
    work = LAGS * portion * across
    return pl.pallas_call(
        functools.partial(correlate_kernel, factor, count, choices, depth),
        out_shape=jax.ShapeDtypeStruct((LAGS, portion, columns), jnp.bfloat16),
        grid_spec=pltpu.PrefetchScalarGridSpec(
            num_scalar_prefetch=1,
            grid=(LAGS,),
            in_specs=in_specs,
            out_specs=pl.BlockSpec((1, portion, across), lambda l, where: (l, 0, where[0])),
            scratch_shapes=[
                pltpu.VMEM((count, length, run), jnp.bfloat16),
                pltpu.SemaphoreType.DMA((count,)),
            ],
        ),
        input_output_aliases=aliases,
        compiler_params=pltpu.CompilerParams(vmem_limit_bytes=20 << 20),
        cost_estimate=pl.CostEstimate(
            flops=2 * work * length,
            bytes_accessed=2 * (work + rows.size + length * across),
            transcendentals=0,
        ),
        name="correlate",
    )(*operands)


def swap(value, axis):
    return lax.ppermute(value, axis, [(0, 1), (1, 0)])


def shards(recordings, filter_taps, slot_table, lag_count):
    segments, channels, width = recordings.shape
    half = channels // 2
    side = lax.axis_index("sub")
    spot = lax.axis_index("row")
    across = lax.axis_index("col")
    row_count = lax.axis_size("row")
    col_count = lax.axis_size("col")
    portion = slot_table.shape[1] // 2
    factor = 1.0 / math.sqrt(segments * width)

    by_time = recordings.transpose(0, 2, 1)
    away = lax.dynamic_slice_in_dim(by_time, (1 - side) * half, half, 2)
    other = swap(away, "sub")
    mine = whiten(by_time, other, filter_taps, side.reshape(1))

    slots = lax.dynamic_slice_in_dim(slot_table[0], side * portion, portion).reshape(portion, 1)
    limits = lax.dynamic_slice_in_dim(
        lag_count.reshape(row_count, col_count, channels), across, 1, 1
    ).reshape(1, -1)

    if half % 128 or col_count != 2:
        whole = lax.all_gather(mine, "sub", axis=1, tiled=True)
        block = lax.all_gather(whole, "col", axis=1, tiled=True)
        rows = build_rows(slots, [block], jnp.zeros((1,), jnp.int32))
        columns = lax.all_gather(whole, "row", axis=1, tiled=True)
        start = jnp.zeros((4,), jnp.int32)
        result = correlate(rows, [[columns]], limits, start, factor, None)
        return result.reshape(LAGS, portion, 1, -1)

    rightward = [(i, i + 1) for i in range(row_count - 1)]
    leftward = [(i + 1, i) for i in range(row_count - 1)]

    def step(left, right):
        return lax.ppermute(left, "row", rightward), lax.ppermute(right, "row", leftward)

    mate = swap(mine, "sub")
    beside = swap(mine, "col")
    arrived = step(mine, mine)
    beside_mate = swap(beside, "sub")
    near, far = across * channels, (1 - across) * channels
    this, that = side * half, (1 - side) * half
    bases = jnp.stack([near + this, near + that, far + this, far + that]).astype(jnp.int32)
    beside, beside_mate, *arrived = lax.optimization_barrier((beside, beside_mate, *arrived))
    lefts, rights = [mine, arrived[0]], [mine, arrived[1]]
    rows = build_rows(slots, [mine, mate, beside, beside_mate], bases)

    def place(source, choice):
        return jnp.stack([source, side, 1 - side, choice]).astype(jnp.int32)

    orders = []
    for z in range(row_count):
        order = []
        for distance in range(1, row_count):
            ends = [(distance, 1), (distance, -1)]
            order += [(d, sign) for d, sign in ends if 0 <= z + sign * d < row_count]
        orders.append(order)

    mates = {}

    def choose(turn):
        kinds = sorted({orders[z][turn] for z in range(row_count)})
        pieces = []
        for distance, sign in kinds:
            piece = (rights if sign > 0 else lefts)[distance]
            if (distance, sign) not in mates:
                mates[distance, sign] = swap(piece, "sub")
            pieces.append([piece, mates[distance, sign]])
        source = choice = jnp.int32(0)
        for z in range(row_count):
            distance, sign = orders[z][turn]
            source = jnp.where(spot == z, z + sign * distance, source)
            choice = jnp.where(spot == z, kinds.index((distance, sign)), choice)
        return pieces, place(source, choice)

    result = None
    group, where = [[mine, mate]], place(spot, jnp.int32(0))
    for turn in range(row_count):
        last = turn == row_count - 1
        ahead = turn + 2 <= row_count - 1
        if ahead:
            arrived = step(lefts[-1], rights[-1])
        if not last:
            following = choose(turn)
        result = correlate(rows, group, limits, where, factor, result)
        if ahead:
            result, *arrived = lax.optimization_barrier((result, *arrived))
            lefts.append(arrived[0])
            rights.append(arrived[1])
        if not last:
            group, where = following
    return result.reshape(LAGS, portion, 1, -1)


def solution(mesh):
    return jax.shard_map(
        shards,
        mesh=mesh,
        in_specs=(P("grp", ("row", "col"), "sub"), P(), P("row", None), P()),
        out_specs=P("grp", ("row", "sub"), "col", None),
        check_vma=False,
    )
```

time: 1730 us -> 164 us (0.09)
  matrix products: 1310 us -> 0 us
  local copies, waits for them, and re-layouts: 166 us -> 2.73 us
  waiting for transfers between devices: 170 us -> 29.1 us
  Pallas kernels: 0 us -> 110 us
  loops' own time: 33.1 us -> 0 us
  other arithmetic: 19.1 us -> 0.38 us
    conv_general_dilated x1 -> x0, matrix products: 1140 us -> none  [shards(): lax.conv_general_dilated(padded.reshape(segments * channels, 1, extent),...]
    dot_general x17 -> x0, matrix products: 170 us -> none  [single_lag(): jnp.einsum('sat,sbt->ab', row_data, shifted, preferred_element_type=jnp.f...]
    all_gather x3 -> x0, waiting for transfers between devices: 168 us -> none  [the longest x1 99.3 us: shards(): segment_cols = lax.all_gather(whole, 'row', axis=1, tiled=True)]
    pallas_call x0 -> x6, Pallas kernels: none -> 110 us  [the longest x4 95.7 us: correlate(): pl.pallas_call(functools.partial(correlate_kernel, factor, count, choices...]
    dynamic_update_slice x34 -> x0, local copies, waits for them, and re-layouts: 74.6 us -> none  [correlate(): return lax.map(single_lag, jnp.arange(lag_total, dtype=jnp.int32))]
    another operation x1 -> x0, loops' own time: 33.1 us -> none  [correlate(): return lax.map(single_lag, jnp.arange(lag_total, dtype=jnp.int32))]
    ppermute x2 -> x16, waiting for transfers between devices: 1.32 us -> 29.1 us  [the longest x10 21.8 us: swap(): return lax.ppermute(value, axis, [(0, 1), (1, 0)])]
    gather x1 -> x0, local copies, waits for them, and re-layouts: 27.3 us -> none  [shards(): row_data = jnp.take(block_rows, chosen, axis=1)]
  transfers between devices with their start and end apart: 5 -> 16, of which waited for: 4 -> 5; matrix products, arithmetic and copies ran while one was open for 3% -> 1% of each run, Pallas kernels for 0% -> 49%
where the time goes in v1:
time: 164 us
  Pallas kernels  110 us (67%)
  waiting for transfers between devices  29.1 us (18%)
  starting transfers between devices  20.9 us (13%)
  local copies, waits for them, and re-layouts  2.73 us (2%)
    pallas_call x4, Pallas kernels, correlate(): pl.pallas_call(functools.partial(correlate_kernel, factor, count, choices...  95.7 us
    ppermute x10, waiting for transfers between devices, swap(): return lax.ppermute(value, axis, [(0, 1), (1, 0)])  21.8 us
    ppermute x3, starting transfers between devices, step(): lax.ppermute(left, 'row', rightward)  11.3 us
    pallas_call x1, Pallas kernels, build_rows(): pl.pallas_call(functools.partial(rows_kernel, len(pieces)), out_shape=jax...  7.74 us
    pallas_call x1, Pallas kernels, whiten(): pl.pallas_call(functools.partial(filter_kernel, samples), out_shape=jax.S...  6.8 us
    ppermute x3, waiting for transfers between devices, step(): lax.ppermute(right, 'row', leftward)  6.1 us
    ppermute x10, starting transfers between devices, swap(): return lax.ppermute(value, axis, [(0, 1), (1, 0)])  5.74 us
    ppermute x3, starting transfers between devices, step(): lax.ppermute(right, 'row', leftward)  3.86 us
  transfers between devices with their start and end apart: 16, of which 5 were waited for; matrix products, arithmetic and copies ran while one was open for 1% of the time, Pallas kernels for 49%

profile of v1, /device:TPU:0, one launch (start us, length us, event | category | flops | bytes accessed | tf_op | source)
XLA Modules:
  0.0 163.6 jit_solution(16890457419613882811)
XLA Ops:
  0.0 1.9 %dynamic-slice_bitcast_fusion = f32[2,1000,256]{2,1,0:T(8,128)S(1)} fusion(f32[2,512,1000]{1,2,0:T(8,128)} %param.4, s32[]{:T(128)S(6)} %select_n.82), kind=kLoop, calls=%fused_computation | loop fusion | bytes 4096004 | tf_op jit(solution)/shard_map/dynamic_slice | solution.py:246
  1.9 0.5 collective-permute-start
  2.4 0.7 pad.4.taps_ref
  3.1 3.0 %collective-permute-done.other_ref = f32[2,1000,256]{2,1,0:T(8,128)S(1)} collective-permute-done((f32[2,1000,256]{2,1,0:T(8,128)S(1)}, f32[2,1000,256]{2,1,0:T(8,128)S(1)}, u32[]{:S(2)}, u32[]{:S(2)}) %collective-permute-start) | collective-permute-done | bytes 2048032 | tf_op jit(solution)/shard_map/ppermute | solution.py:231
  6.1 6.8 %whiten.1 = bf16[8,2,128,256]{3,2,1,0:T(8,128)(2,1)S(1)} custom-call(s32[1]{0:T(128)} %bitcast.1.side_ref, f32[2,1000,512]{2,1,0:T(8,128)S(1)} %bitcast.24, f32[2,1000,256]{2,1,0:T(8,128)S(1)} %collective-permute-done.other_ref, f32[1,384]{1,0:T(1,128)S(1)} %pad.4.taps_ref), custom_call_target="tpu_custom_call" | custom-call | tf_op jit(solution)/shard_map/whiten/pallas_call | solution.py:80
  12.9 2.9 %collective-permute-start.2 = (bf16[2048,256]{1,0:T(8,128)(2,1)S(1)}, bf16[2048,256]{1,0:T(8,128)(2,1)}, u32[]{:S(2)}, u32[]{:S(2)}) collective-permute-start(bf16[2048,256]{1,0:T(8,128)(2,1)S(1)} %bitcast.25), channel_id=1, source_target_pairs={{0,2},{2,0},{1,3},{3,1},{4,6},{6,4},{5,7},{7,5},{8,10},{10,8},{9,1... | collective-permute-start | bytes 3145736 | tf_op jit(solution)/shard_map/ppermute | solution.py:231
  15.9 3.5 %collective-permute-start.4 = (bf16[2048,256]{1,0:T(8,128)(2,1)S(1)}, bf16[2048,256]{1,0:T(8,128)(2,1)S(1)}, u32[]{:S(2)}, u32[]{:S(2)}) collective-permute-start(bf16[2048,256]{1,0:T(8,128)(2,1)S(1)} %bitcast.26), channel_id=1, source_target_pairs={{0,4},{4,8},{8,12},{1,5},{5,9},{9,13},{2,6},{6,10},{10,14},{3,7},{... | collective-permute-start | bytes 3145736 | tf_op jit(solution)/shard_map/ppermute | solution.py:268
  19.4 1.3 collective-permute-start.5
  20.7 18.7 %collective-permute-done.2.refs_2_ = bf16[2048,256]{1,0:T(8,128)(2,1)} collective-permute-done((bf16[2048,256]{1,0:T(8,128)(2,1)S(1)}, bf16[2048,256]{1,0:T(8,128)(2,1)}, u32[]{:S(2)}, u32[]{:S(2)}) %collective-permute-start.2) | collective-permute-done | bytes 1048608 | tf_op jit(solution)/shard_map/ppermute | solution.py:231
  40.6 1.2 collective-permute-done.4.refs_0_
  41.8 4.2 %collective-permute-done.5.refs_2_ = bf16[2048,256]{1,0:T(8,128)(2,1)S(1)} collective-permute-done((bf16[2048,256]{1,0:T(8,128)(2,1)S(1)}, bf16[2048,256]{1,0:T(8,128)(2,1)S(1)}, u32[]{:S(2)}, u32[]{:S(2)}) %collective-permute-start.5) | collective-permute-done | bytes 1048608 | tf_op jit(solution)/shard_map/ppermute | solution.py:268
  45.9 3.5 %collective-permute-start.6 = (bf16[2048,256]{1,0:T(8,128)(2,1)S(1)}, bf16[2048,256]{1,0:T(8,128)(2,1)S(1)}, u32[]{:S(2)}, u32[]{:S(2)}) collective-permute-start(bf16[2048,256]{1,0:T(8,128)(2,1)S(1)} %collective-permute-done.4.refs_0_), channel_id=1, source_target_pairs={{0,4},{4,8},{8,12},{1,5},{5,9},{9,13},{2,6},{6,10},{10,14},{3,7},{... | collective-permute-start | bytes 3145736 | tf_op jit(solution)/shard_map/ppermute | solution.py:268
  49.5 1.3 collective-permute-start.7
  50.8 0.6 collective-permute-start.11
  51.3 7.7 %rows.1.rows_ref = bf16[512,6144]{1,0:T(8,128)(2,1)S(1)} custom-call(s32[4]{0:T(128)S(1)} %pad_add_fusion.1.base_ref, s32[512,1]{1,0:T(8,128)S(1)} %copy.9.slots_ref, bf16[2048,256]{1,0:T(8,128)(2,1)S(1)} %bitcast.29, bf16[2048,256]{1,0:T(8,128)(2,1)} %collective-permute-done.1.refs_1_, bf16[2048,256]{1,0:T(8,128)(2,1)} %collective-permute-done.2.refs_2_, ...), custom_call_target="tpu_custom_call" | custom-call | tf_op jit(solution)/shard_map/rows/pallas_call | solution.py:133
  59.1 24.8 %correlate.4.refs_4_ = bf16[17,512,2048]{2,1,0:T(8,128)(2,1)} custom-call(s32[4]{0:T(128)S(1)} %pad_add_fusion.2.where_ref, bf16[512,6144]{1,0:T(8,128)(2,1)S(1)} %rows.1.rows_ref, s32[1,2048]{1,0:T(1,128)S(1)} %bitcast.31, bf16[2048,256]{1,0:T(8,128)(2,1)S(1)} %bitcast.30, bf16[2048,256]{1,0:T(8,128)(2,1)} %collective-permute-done.1.refs_1_), custom_call_target="tpu_custom_call" | custom-call | flops 18253611008 | bytes 17301504 | tf_op jit(solution)/shard_map/correlate/pallas_call | solution.py:206
  83.9 4.3 %collective-permute-start.12 = (bf16[2048,256]{1,0:T(8,128)(2,1)S(1)}, bf16[2048,256]{1,0:T(8,128)(2,1)S(1)}, u32[]{:S(2)}, u32[]{:S(2)}) collective-permute-start(bf16[2048,256]{1,0:T(8,128)(2,1)S(1)} %collective-permute-done.6.refs_2_.refs_0_), channel_id=1, source_target_pairs={{0,4},{4,8},{8,12},{1,5},{5,9},{9,13},{2,6},{6,10},{10,14},{3,7},{... | collective-permute-start | bytes 3145736 | tf_op jit(solution)/shard_map/ppermute | solution.py:268
  88.3 1.3 collective-permute-start.13
  89.6 0.5 collective-permute-start.9
  90.2 23.6 %correlate.5.refs_6_ = bf16[17,512,2048]{2,1,0:T(8,128)(2,1)} custom-call(s32[4]{0:T(128)S(1)} %pad_add_fusion.3.where_ref, bf16[512,6144]{1,0:T(8,128)(2,1)S(1)} %rows.1.rows_ref, s32[1,2048]{1,0:T(1,128)S(1)} %bitcast.32, bf16[2048,256]{1,0:T(8,128)(2,1)S(1)} %collective-permute-done.4.refs_0_, ...), custom_call_target="tpu_custom_call", output_to_operand_aliasing={{}: (7, {})} | custom-call | flops 18253611008 | bytes 17301504 | tf_op jit(solution)/shard_map/correlate/pallas_call | solution.py:206
  113.8 1.9 %collective-permute-done.13.refs_6_ = bf16[2048,256]{1,0:T(8,128)(2,1)S(1)} collective-permute-done((bf16[2048,256]{1,0:T(8,128)(2,1)S(1)}, bf16[2048,256]{1,0:T(8,128)(2,1)S(1)}, u32[]{:S(2)}, u32[]{:S(2)}) %collective-permute-start.13) | collective-permute-done | bytes 1048608 | tf_op jit(solution)/shard_map/ppermute | solution.py:268
  115.8 0.5 collective-permute-start.15
  116.3 23.7 %correlate.6.refs_8_ = bf16[17,512,2048]{2,1,0:T(8,128)(2,1)} custom-call(s32[4]{0:T(128)S(1)} %pad_add_fusion.4.where_ref, bf16[512,6144]{1,0:T(8,128)(2,1)S(1)} %rows.1.rows_ref, s32[1,2048]{1,0:T(1,128)S(1)} %bitcast.33, bf16[2048,256]{1,0:T(8,128)(2,1)S(1)} %collective-permute-done.4.refs_0_, ...), custom_call_target="tpu_custom_call", output_to_operand_aliasing={{}: (9, {})} | custom-call | flops 18253611008 | bytes 17301504 | tf_op jit(solution)/shard_map/correlate/pallas_call | solution.py:206
  140.0 23.7 %correlate.7 = bf16[17,512,2048]{2,1,0:T(8,128)(2,1)} custom-call(s32[4]{0:T(128)S(1)} %pad_add_fusion.where_ref, bf16[512,6144]{1,0:T(8,128)(2,1)S(1)} %rows.1.rows_ref, s32[1,2048]{1,0:T(1,128)S(1)} %bitcast.34, bf16[2048,256]{1,0:T(8,128)(2,1)S(1)} %collective-permute-done.6.refs_2_.refs_0_, ...), custom_call_target="tpu_custom_call", output_to_operand_aliasing={{}: (11, {})} | custom-call | flops 18253611008 | bytes 17301504 | tf_op jit(solution)/shard_map/correlate/pallas_call | solution.py:206
  (33 shorter events, 1.3 us)
Async XLA Ops:
  0.0 39.9 %copy-start = (s32[1,1024]{1,0:T(1,128)S(1)}, s32[1,1024]{1,0:T(1,128)}, u32[]{:S(2)}) copy-start(s32[1,1024]{1,0:T(1,128)} %param.6) | copy-start | bytes 12292
  0.0 40.1 %copy-start.3 = (s32[4096]{0:T(1024)S(1)}, s32[4096]{0:T(1024)}, u32[]{:S(2)}) copy-start(s32[4096]{0:T(1024)} %param.7) | copy-start | bytes 49156
  0.0 6.1 %copy-start.2 = (f32[2,512,1000]{1,2,0:T(8,128)S(1)}, f32[2,512,1000]{1,2,0:T(8,128)}, u32[]{:S(2)}) copy-start(f32[2,512,1000]{1,2,0:T(8,128)} %param.4) | copy-start | bytes 12288004
  1.9 4.2 %collective-permute-start = (f32[2,1000,256]{2,1,0:T(8,128)S(1)}, f32[2,1000,256]{2,1,0:T(8,128)S(1)}, u32[]{:S(2)}, u32[]{:S(2)}) collective-permute-start(f32[2,1000,256]{2,1,0:T(8,128)S(1)} %dynamic-slice_bitcast_fusion), channel_id=1, source_target_pairs={{0,1},{1,0},{2,3},{3,2},{4,5},{5,4},{6,7},{7,6},{8,9},{9,8},{10,11... | collective-permute-start | bytes 6144008 | tf_op jit(solution)/shard_map/ppermute | solution.py:231
  12.9 26.5 %collective-permute-start.2 = (bf16[2048,256]{1,0:T(8,128)(2,1)S(1)}, bf16[2048,256]{1,0:T(8,128)(2,1)}, u32[]{:S(2)}, u32[]{:S(2)}) collective-permute-start(bf16[2048,256]{1,0:T(8,128)(2,1)S(1)} %bitcast.25), channel_id=1, source_target_pairs={{0,2},{2,0},{1,3},{3,1},{4,6},{6,4},{5,7},{7,5},{8,10},{10,8},{9,1... | collective-permute-start | bytes 3145736 | tf_op jit(solution)/shard_map/ppermute | solution.py:231
  15.9 25.9 %collective-permute-start.4 = (bf16[2048,256]{1,0:T(8,128)(2,1)S(1)}, bf16[2048,256]{1,0:T(8,128)(2,1)S(1)}, u32[]{:S(2)}, u32[]{:S(2)}) collective-permute-start(bf16[2048,256]{1,0:T(8,128)(2,1)S(1)} %bitcast.26), channel_id=1, source_target_pairs={{0,4},{4,8},{8,12},{1,5},{5,9},{9,13},{2,6},{6,10},{10,14},{3,7},{... | collective-permute-start | bytes 3145736 | tf_op jit(solution)/shard_map/ppermute | solution.py:268
  19.4 26.5 %collective-permute-start.5 = (bf16[2048,256]{1,0:T(8,128)(2,1)S(1)}, bf16[2048,256]{1,0:T(8,128)(2,1)S(1)}, u32[]{:S(2)}, u32[]{:S(2)}) collective-permute-start(bf16[2048,256]{1,0:T(8,128)(2,1)S(1)} %bitcast.27), channel_id=1, source_target_pairs={{4,0},{8,4},{12,8},{5,1},{9,5},{13,9},{6,2},{10,6},{14,10},{7,3},{... | collective-permute-start | bytes 3145736 | tf_op jit(solution)/shard_map/ppermute | solution.py:268
  39.4 6.5 %collective-permute-start.3 = (bf16[2048,256]{1,0:T(8,128)(2,1)}, bf16[2048,256]{1,0:T(8,128)(2,1)}, u32[]{:S(2)}, u32[]{:S(2)}) collective-permute-start(bf16[2048,256]{1,0:T(8,128)(2,1)} %collective-permute-done.2.refs_2_), channel_id=1, source_target_pairs={{0,1},{1,0},{2,3},{3,2},{4,5},{5,4},{6,7},{7,6},{8,9},{9,8},{10,11... | collective-permute-start | bytes 3145736 | tf_op jit(solution)/shard_map/ppermute | solution.py:231
  39.4 11.9 %collective-permute-start.1 = (bf16[2048,256]{1,0:T(8,128)(2,1)S(1)}, bf16[2048,256]{1,0:T(8,128)(2,1)}, u32[]{:S(2)}, u32[]{:S(2)}) collective-permute-start(bf16[2048,256]{1,0:T(8,128)(2,1)S(1)} %bitcast.28), channel_id=1, source_target_pairs={{0,1},{1,0},{2,3},{3,2},{4,5},{5,4},{6,7},{7,6},{8,9},{9,8},{10,11... | collective-permute-start | bytes 3145736 | tf_op jit(solution)/shard_map/ppermute | solution.py:231
  45.9 37.9 %collective-permute-start.6 = (bf16[2048,256]{1,0:T(8,128)(2,1)S(1)}, bf16[2048,256]{1,0:T(8,128)(2,1)S(1)}, u32[]{:S(2)}, u32[]{:S(2)}) collective-permute-start(bf16[2048,256]{1,0:T(8,128)(2,1)S(1)} %collective-permute-done.4.refs_0_), channel_id=1, source_target_pairs={{0,4},{4,8},{8,12},{1,5},{5,9},{9,13},{2,6},{6,10},{10,14},{3,7},{... | collective-permute-start | bytes 3145736 | tf_op jit(solution)/shard_map/ppermute | solution.py:268
  49.4 40.2 %collective-permute-start.10 = (bf16[2048,256]{1,0:T(8,128)(2,1)S(1)}, bf16[2048,256]{1,0:T(8,128)(2,1)S(1)}, u32[]{:S(2)}, u32[]{:S(2)}) collective-permute-start(bf16[2048,256]{1,0:T(8,128)(2,1)S(1)} %collective-permute-done.4.refs_0_), channel_id=1, source_target_pairs={{0,1},{1,0},{2,3},{3,2},{4,5},{5,4},{6,7},{7,6},{8,9},{9,8},{10,11... | collective-permute-start | bytes 3145736 | tf_op jit(solution)/shard_map/ppermute | solution.py:231
  49.5 34.4 %collective-permute-start.7 = (bf16[2048,256]{1,0:T(8,128)(2,1)S(1)}, bf16[2048,256]{1,0:T(8,128)(2,1)S(1)}, u32[]{:S(2)}, u32[]{:S(2)}) collective-permute-start(bf16[2048,256]{1,0:T(8,128)(2,1)S(1)} %collective-permute-done.5.refs_2_), channel_id=1, source_target_pairs={{4,0},{8,4},{12,8},{5,1},{9,5},{13,9},{6,2},{10,6},{14,10},{7,3},{... | collective-permute-start | bytes 3145736 | tf_op jit(solution)/shard_map/ppermute | solution.py:268
  50.8 39.4 %collective-permute-start.11 = (bf16[2048,256]{1,0:T(8,128)(2,1)S(1)}, bf16[2048,256]{1,0:T(8,128)(2,1)S(1)}, u32[]{:S(2)}, u32[]{:S(2)}) collective-permute-start(bf16[2048,256]{1,0:T(8,128)(2,1)S(1)} %collective-permute-done.5.refs_2_), channel_id=1, source_target_pairs={{0,1},{1,0},{2,3},{3,2},{4,5},{5,4},{6,7},{7,6},{8,9},{9,8},{10,11... | collective-permute-start | bytes 3145736 | tf_op jit(solution)/shard_map/ppermute | solution.py:231
  83.9 29.9 %collective-permute-start.12 = (bf16[2048,256]{1,0:T(8,128)(2,1)S(1)}, bf16[2048,256]{1,0:T(8,128)(2,1)S(1)}, u32[]{:S(2)}, u32[]{:S(2)}) collective-permute-start(bf16[2048,256]{1,0:T(8,128)(2,1)S(1)} %collective-permute-done.6.refs_2_.refs_0_), channel_id=1, source_target_pairs={{0,4},{4,8},{8,12},{1,5},{5,9},{9,13},{2,6},{6,10},{10,14},{3,7},{... | collective-permute-start | bytes 3145736 | tf_op jit(solution)/shard_map/ppermute | solution.py:268
  88.2 28.0 %collective-permute-start.8 = (bf16[2048,256]{1,0:T(8,128)(2,1)S(1)}, bf16[2048,256]{1,0:T(8,128)(2,1)S(1)}, u32[]{:S(2)}, u32[]{:S(2)}) collective-permute-start(bf16[2048,256]{1,0:T(8,128)(2,1)S(1)} %collective-permute-done.6.refs_2_.refs_0_), channel_id=1, source_target_pairs={{0,1},{1,0},{2,3},{3,2},{4,5},{5,4},{6,7},{7,6},{8,9},{9,8},{10,11... | collective-permute-start | bytes 3145736 | tf_op jit(solution)/shard_map/ppermute | solution.py:231
  88.3 27.4 %collective-permute-start.13 = (bf16[2048,256]{1,0:T(8,128)(2,1)S(1)}, bf16[2048,256]{1,0:T(8,128)(2,1)S(1)}, u32[]{:S(2)}, u32[]{:S(2)}) collective-permute-start(bf16[2048,256]{1,0:T(8,128)(2,1)S(1)} %collective-permute-done.7.refs_4_.refs_2_), channel_id=1, source_target_pairs={{4,0},{8,4},{12,8},{5,1},{9,5},{13,9},{6,2},{10,6},{14,10},{7,3},{... | collective-permute-start | bytes 3145736 | tf_op jit(solution)/shard_map/ppermute | solution.py:268
  89.6 26.6 %collective-permute-start.9 = (bf16[2048,256]{1,0:T(8,128)(2,1)S(1)}, bf16[2048,256]{1,0:T(8,128)(2,1)S(1)}, u32[]{:S(2)}, u32[]{:S(2)}) collective-permute-start(bf16[2048,256]{1,0:T(8,128)(2,1)S(1)} %collective-permute-done.7.refs_4_.refs_2_), channel_id=1, source_target_pairs={{0,1},{1,0},{2,3},{3,2},{4,5},{5,4},{6,7},{7,6},{8,9},{9,8},{10,11... | collective-permute-start | bytes 3145736 | tf_op jit(solution)/shard_map/ppermute | solution.py:231
  115.8 24.2 %collective-permute-start.14 = (bf16[2048,256]{1,0:T(8,128)(2,1)S(1)}, bf16[2048,256]{1,0:T(8,128)(2,1)S(1)}, u32[]{:S(2)}, u32[]{:S(2)}) collective-permute-start(bf16[2048,256]{1,0:T(8,128)(2,1)S(1)} %collective-permute-done.12.refs_4_), channel_id=1, source_target_pairs={{0,1},{1,0},{2,3},{3,2},{4,5},{5,4},{6,7},{7,6},{8,9},{9,8},{10,11... | collective-permute-start | bytes 3145736 | tf_op jit(solution)/shard_map/ppermute | solution.py:231
  115.8 24.2 %collective-permute-start.15 = (bf16[2048,256]{1,0:T(8,128)(2,1)S(1)}, bf16[2048,256]{1,0:T(8,128)(2,1)S(1)}, u32[]{:S(2)}, u32[]{:S(2)}) collective-permute-start(bf16[2048,256]{1,0:T(8,128)(2,1)S(1)} %collective-permute-done.13.refs_6_), channel_id=1, source_target_pairs={{0,1},{1,0},{2,3},{3,2},{4,5},{5,4},{6,7},{7,6},{8,9},{9,8},{10,11... | collective-permute-start | bytes 3145736 | tf_op jit(solution)/shard_map/ppermute | solution.py:231
  140.0 23.7 %copy-start.1 = (s32[1,1024]{1,0:T(1,128)S(1)}, s32[1,1024]{1,0:T(1,128)}, u32[]{:S(2)}) copy-start(s32[1,1024]{1,0:T(1,128)} %param.6) | copy-start | bytes 12292

commit v2 on v1

--- a/solution.py
+++ b/solution.py
@@ -100,19 +100,67 @@
     return out.reshape(PHASES * segments * SLOTS, half)
 
 
+def row_blocks():
+    blocks = [[(j, 1)] for j in range(PHASES)]
+
+    def minus(a, b):
+        return a + [(index, -sign) for index, sign in b]
+
+    def outer(kind, k):
+        even, odd, after = [(1 + 2 * k, 1)], [(2 + 2 * k, 1)], [(3 + 2 * k, 1)]
+        return [minus(even, odd), odd, minus(after, odd)][kind]
+
+    blocks += [outer(1, k) for k in range(PHASES + 3)]
+    for first in (0, 2):
+        for second in range(3):
+            for k in range(5):
+                even, odd = outer(first, 2 * k), outer(first, 2 * k + 1)
+                if second == 0:
+                    blocks.append(minus(even, odd))
+                elif second == 1:
+                    blocks.append(odd)
+                else:
+                    blocks.append(minus(outer(first, 2 * k + 2), odd))
+    return blocks
+
+
+def column_blocks():
+    blocks = [[2 * k, 2 * k + 1] for k in range(4)]
+    for first in (0, 1):
+        for second in ([0], [0, 2], [2]):
+            blocks += [[4 * k + first + b for b in second] for k in range(2)]
+    return blocks
+
+
+ROW_BLOCKS = PHASES + PHASES + 3 + 30
+COLUMN_BLOCKS = 16
+
+
 def rows_kernel(count, base_ref, slots_ref, *refs):
-    pieces, out_ref = refs[:count], refs[count]
+    pieces, out_ref, pick, shifted = refs[:count], refs[count], refs[count + 1], refs[count + 2]
     phase = pl.program_id(0)
     rows = slots_ref.shape[0]
+    depth = pieces[0].shape[0]
+
+    @pl.when(phase == 0)
+    def _():
+        first = 0
+        for k, piece in enumerate(pieces):
+            width = piece.shape[1]
+            channel = lax.broadcasted_iota(jnp.int32, (rows, width), 1) + base_ref[k]
+            chosen = (slots_ref[...] == channel).astype(jnp.float32).astype(jnp.bfloat16)
+            pick[:, first : first + width] = chosen
+            first += width
+
     total = None
-    for k, piece in enumerate(pieces):
+    first = 0
+    for piece in pieces:
         width = piece.shape[1]
-        channel = lax.broadcasted_iota(jnp.int32, (rows, width), 1) + base_ref[k]
-        pick = (slots_ref[...] == channel).astype(jnp.float32).astype(jnp.bfloat16)
-        term = nt_dot(pick, piece[...])
+        term = nt_dot(pick[:, first : first + width], piece[...])
+        first += width
         total = term if total is None else total + term
-    depth = total.shape[1]
     for carry in range(3):
+        moved = total
         if carry:
             moved = jnp.concatenate(
                 [
@@ -121,10 +169,21 @@
                 ],
                 axis=1,
             )
-        else:
-            moved = total
-        start = pl.multiple_of((2 - carry) * PHASES * depth + phase * depth, depth)
-        out_ref[:, pl.ds(start, depth)] = moved.astype(jnp.bfloat16)
+        shifted[(2 - carry) * PHASES + phase] = moved.astype(jnp.bfloat16)
+
+    @pl.when(phase == PHASES - 1)
+    def _():
+        def block(terms):
+            if len(terms) == 1:
+                return shifted[terms[0][0]]
+            value = None
+            for index, sign in terms:
+                part = shifted[index].astype(jnp.float32) * sign
+                value = part if value is None else value + part
+            return value.astype(jnp.bfloat16)
+
+        for slot, terms in enumerate(row_blocks()):
+            out_ref[:, slot * depth : (slot + 1) * depth] = block(terms)
 
 
 def build_rows(slots, pieces, bases):
@@ -132,25 +191,33 @@
     depth = pieces[0].shape[0] // PHASES
     return pl.pallas_call(
         functools.partial(rows_kernel, len(pieces)),
-        out_shape=jax.ShapeDtypeStruct((rows, 3 * PHASES * depth), jnp.bfloat16),
+        out_shape=jax.ShapeDtypeStruct((rows, ROW_BLOCKS * depth), jnp.bfloat16),
         grid_spec=pltpu.PrefetchScalarGridSpec(
             num_scalar_prefetch=1,
             grid=(PHASES,),
             in_specs=[pl.BlockSpec((rows, 1), lambda j, base: (0, 0))]
             + [pl.BlockSpec((depth, p.shape[1]), lambda j, base: (j, 0)) for p in pieces],
-            out_specs=pl.BlockSpec((rows, 3 * PHASES * depth), lambda j, base: (0, 0)),
+            out_specs=pl.BlockSpec(
+                (rows, ROW_BLOCKS * depth), lambda j, base: (0, 0), pipeline_mode=pl.Buffered(1)
+            ),
+            scratch_shapes=[
+                pltpu.VMEM((rows, sum(p.shape[1] for p in pieces)), jnp.bfloat16),
+                pltpu.VMEM((3 * PHASES, rows, depth), jnp.bfloat16),
+            ],
         ),
-        compiler_params=pltpu.CompilerParams(vmem_limit_bytes=24 << 20),
+        compiler_params=pltpu.CompilerParams(vmem_limit_bytes=36 << 20),
         name="rows",
     )(bases, slots, *pieces)
 
 
 def correlate_kernel(factor, count, choices, depth, where_ref, rows_ref, limit_ref, *refs):
-    pieces, out_ref, held, done = refs[: count * choices], refs[-3], refs[-2], refs[-1]
-    lag = pl.program_id(0)
+    pieces = refs[: count * choices]
+    out_ref, held, sums, done = refs[-4:]
+    step = pl.program_id(0)
     length = PHASES * depth
-
-    @pl.when(lag == 0)
+    width = held.shape[2]
+
+    @pl.when(step == 0)
     def _():
         for choice in range(choices):
 
@@ -165,27 +232,62 @@
                 for copy in copies:
                     copy.wait()
 
-    start = pl.multiple_of((LAGS - 1 - lag) * depth, depth)
-    rows = rows_ref[:, pl.ds(start, length)]
-    width = held.shape[2]
+        for k in range(count):
+            for slot, phases in enumerate(column_blocks()):
+                value = None
+                for phase in phases:
+                    part = held[k, phase * depth : (phase + 1) * depth].astype(jnp.float32)
+                    value = part if value is None else value + part
+                sums[k, slot * depth : (slot + 1) * depth] = value.astype(jnp.bfloat16)
+
     block = min(width, 256)
     for k in range(count):
         for first in range(0, width, block):
             spot = first
             if count > 1:
                 spot = pl.multiple_of(where_ref[1 + k] * width + first, block)
-            product = jnp.dot(
-                rows, held[k, :, first : first + block], preferred_element_type=jnp.float32
-            )
-            keep = lag < limit_ref[:, pl.ds(spot, block)]
-            out_ref[0, :, pl.ds(spot, block)] = jnp.where(keep, product * factor, 0.0).astype(
-                jnp.bfloat16
-            )
+            limit = limit_ref[:, pl.ds(spot, block)]
+
+            def write(slot, lag, product, spot=spot, limit=limit):
+                value = jnp.where(lag < limit, product, 0.0)
+                out_ref[slot, :, pl.ds(spot, block)] = value.astype(jnp.bfloat16)
+
+            @pl.when(step < 4)
+            def _():
+                quad = 3 - step
+
+                def product(row_slot, column_slot, length):
+                    start = pl.multiple_of(row_slot * depth, depth)
+                    return factor * nn_dot(
+                        rows_ref[:, pl.ds(start, length * depth)],
+                        sums[
+                            k,
+                            column_slot * depth : (column_slot + length) * depth,
+                            first : first + block,
+                        ],
+                    )
+
+                shared = [product(PHASES + 2 * quad + half, 0, 4) for half in range(2)]
+                for outer, near in ((0, 0), (1, 1)):
+
+                    def inner(kind):
+                        index = 3 * outer + kind
+                        return product(2 * PHASES + 3 + 5 * index + quad, 4 + 2 * index, 2)
+
+                    middle = inner(1)
+                    for half in range(2):
+                        slot = 3 - 2 * half - near
+                        write(slot, 4 * step + slot, shared[half] + (middle + inner(2 * half)))
+
+            @pl.when(step == 4)
+            def _():
+                rows = rows_ref[:, :length]
+                write(0, LAGS - 1, factor * nn_dot(rows, held[k, :, first : first + block]))
 
 
 def correlate(rows, pieces, limits, where, factor, buffer):
     choices, count = len(pieces), len(pieces[0])
-    depth = rows.shape[1] // (3 * PHASES)
+    depth = rows.shape[1] // ROW_BLOCKS
     length = PHASES * depth
     portion = rows.shape[0]
     columns = limits.shape[1]
@@ -208,16 +310,17 @@
         out_shape=jax.ShapeDtypeStruct((LAGS, portion, columns), jnp.bfloat16),
         grid_spec=pltpu.PrefetchScalarGridSpec(
             num_scalar_prefetch=1,
-            grid=(LAGS,),
+            grid=(pl.cdiv(LAGS, 4),),
             in_specs=in_specs,
-            out_specs=pl.BlockSpec((1, portion, across), lambda l, where: (l, 0, where[0])),
+            out_specs=pl.BlockSpec((4, portion, across), lambda l, where: (l, 0, where[0])),
             scratch_shapes=[
                 pltpu.VMEM((count, length, run), jnp.bfloat16),
+                pltpu.VMEM((count, COLUMN_BLOCKS * depth, run), jnp.bfloat16),
                 pltpu.SemaphoreType.DMA((count,)),
             ],
         ),
         input_output_aliases=aliases,
-        compiler_params=pltpu.CompilerParams(vmem_limit_bytes=20 << 20),
+        compiler_params=pltpu.CompilerParams(vmem_limit_bytes=24 << 20),
         cost_estimate=pl.CostEstimate(
             flops=2 * work * length,
             bytes_accessed=2 * (work + rows.size + length * across),

time: 164 us -> 152 us (0.927)
  Pallas kernels: 110 us -> 88.9 us
  waiting for transfers between devices: 29.1 us -> 34.6 us
  local copies, waits for them, and re-layouts: 2.73 us -> 5.47 us
    pallas_call x4, Pallas kernels: 95.7 us -> 70 us  [correlate(): pl.pallas_call(functools.partial(correlate_kernel, factor, count, choices...]
    pallas_call x1, Pallas kernels: 7.74 us -> 12.1 us  [build_rows(): pl.pallas_call(functools.partial(rows_kernel, len(pieces)), out_shape=jax...]
    ppermute x3, waiting for transfers between devices: 1.17 us -> 3.99 us  [step(): lax.ppermute(left, 'row', rightward)]
    ppermute x3, waiting for transfers between devices: 6.1 us -> 8.88 us  [step(): lax.ppermute(right, 'row', leftward)]
    unnamed x8 -> x6, local copies, waits for them, and re-layouts: 0.02 us -> 2.17 us
  transfers between devices with their start and end apart: 16 -> 16, of which waited for: 5 -> 6; matrix products, arithmetic and copies ran while one was open for 1% -> 1% of each run, Pallas kernels for 49% -> 43%
where the time goes in v2:
time: 152 us; the launch traced here: 151 us
  Pallas kernels  88.9 us (58%)
  waiting for transfers between devices  34.6 us (23%)
  starting transfers between devices  21.3 us (14%)
  local copies, waits for them, and re-layouts  5.47 us (4%)
    pallas_call x4, Pallas kernels, correlate(): pl.pallas_call(functools.partial(correlate_kernel, factor, count, choices...  70 us
    ppermute x10, waiting for transfers between devices, swap(): return lax.ppermute(value, axis, [(0, 1), (1, 0)])  21.8 us
    pallas_call x1, Pallas kernels, build_rows(): pl.pallas_call(functools.partial(rows_kernel, len(pieces)), out_shape=jax...  12.1 us
    ppermute x3, starting transfers between devices, step(): lax.ppermute(left, 'row', rightward)  11.3 us
    ppermute x3, waiting for transfers between devices, step(): lax.ppermute(right, 'row', leftward)  8.88 us
    pallas_call x1, Pallas kernels, whiten(): pl.pallas_call(functools.partial(filter_kernel, samples), out_shape=jax.S...  6.8 us
    ppermute x10, starting transfers between devices, swap(): return lax.ppermute(value, axis, [(0, 1), (1, 0)])  5.73 us
    ppermute x3, starting transfers between devices, step(): lax.ppermute(right, 'row', leftward)  4.27 us
  transfers between devices with their start and end apart: 16, of which 6 were waited for; matrix products, arithmetic and copies ran while one was open for 1% of the time, Pallas kernels for 43%

profile of v2, /device:TPU:0, one launch (start us, length us, event | category | flops | bytes accessed | tf_op | source)
XLA Modules:
  0.0 151.2 jit_solution(16205687635364609623)
XLA Ops:
  0.0 1.7 %dynamic-slice_bitcast_fusion = f32[2,1000,256]{2,1,0:T(8,128)S(1)} fusion(f32[2,512,1000]{1,2,0:T(8,128)} %param.4, s32[]{:T(128)S(6)} %select_n.82), kind=kLoop, calls=%fused_computation | loop fusion | bytes 4096004 | tf_op jit(solution)/shard_map/dynamic_slice | solution.py:349
  2.2 0.7 pad.4.taps_ref
  2.9 3.0 %collective-permute-done.other_ref = f32[2,1000,256]{2,1,0:T(8,128)S(1)} collective-permute-done((f32[2,1000,256]{2,1,0:T(8,128)S(1)}, f32[2,1000,256]{2,1,0:T(8,128)S(1)}, u32[]{:S(2)}, u32[]{:S(2)}) %collective-permute-start) | collective-permute-done | bytes 2048032 | tf_op jit(solution)/shard_map/ppermute | solution.py:334
  6.0 2.2 %copy-done.2 = f32[2,512,1000]{1,2,0:T(8,128)S(1)} copy-done((f32[2,512,1000]{1,2,0:T(8,128)S(1)}, f32[2,512,1000]{1,2,0:T(8,128)}, u32[]{:S(2)}) %copy-start.2) | copy-done | bytes 4096024
  8.1 6.8 %whiten.1 = bf16[8,2,128,256]{3,2,1,0:T(8,128)(2,1)S(1)} custom-call(s32[1]{0:T(128)} %bitcast.1.side_ref, f32[2,1000,512]{2,1,0:T(8,128)S(1)} %bitcast.24, f32[2,1000,256]{2,1,0:T(8,128)S(1)} %collective-permute-done.other_ref, f32[1,384]{1,0:T(1,128)S(1)} %pad.4.taps_ref), custom_call_target="tpu_custom_call" | custom-call | tf_op jit(solution)/shard_map/whiten/pallas_call | solution.py:80
  14.9 2.9 %collective-permute-start.2 = (bf16[2048,256]{1,0:T(8,128)(2,1)S(1)}, bf16[2048,256]{1,0:T(8,128)(2,1)}, u32[]{:S(2)}, u32[]{:S(2)}) collective-permute-start(bf16[2048,256]{1,0:T(8,128)(2,1)S(1)} %bitcast.25), channel_id=1, source_target_pairs={{0,2},{2,0},{1,3},{3,1},{4,6},{6,4},{5,7},{7,5},{8,10},{10,8},{9,1... | collective-permute-start | bytes 3145736 | tf_op jit(solution)/shard_map/ppermute | solution.py:334
  17.9 3.5 %collective-permute-start.4 = (bf16[2048,256]{1,0:T(8,128)(2,1)S(1)}, bf16[2048,256]{1,0:T(8,128)(2,1)S(1)}, u32[]{:S(2)}, u32[]{:S(2)}) collective-permute-start(bf16[2048,256]{1,0:T(8,128)(2,1)S(1)} %bitcast.26), channel_id=1, source_target_pairs={{0,4},{4,8},{8,12},{1,5},{5,9},{9,13},{2,6},{6,10},{10,14},{3,7},{... | collective-permute-start | bytes 3145736 | tf_op jit(solution)/shard_map/ppermute | solution.py:371
  21.4 1.3 collective-permute-start.5
  22.7 18.7 %collective-permute-done.2.refs_2_ = bf16[2048,256]{1,0:T(8,128)(2,1)} collective-permute-done((bf16[2048,256]{1,0:T(8,128)(2,1)S(1)}, bf16[2048,256]{1,0:T(8,128)(2,1)}, u32[]{:S(2)}, u32[]{:S(2)}) %collective-permute-start.2) | collective-permute-done | bytes 1048608 | tf_op jit(solution)/shard_map/ppermute | solution.py:334
  42.1 0.7 reshape.24
  43.8 4.2 %collective-permute-done.5.refs_2_ = bf16[2048,256]{1,0:T(8,128)(2,1)S(1)} collective-permute-done((bf16[2048,256]{1,0:T(8,128)(2,1)S(1)}, bf16[2048,256]{1,0:T(8,128)(2,1)S(1)}, u32[]{:S(2)}, u32[]{:S(2)}) %collective-permute-start.5) | collective-permute-done | bytes 1048608 | tf_op jit(solution)/shard_map/ppermute | solution.py:371
  47.9 3.5 %collective-permute-start.6 = (bf16[2048,256]{1,0:T(8,128)(2,1)S(1)}, bf16[2048,256]{1,0:T(8,128)(2,1)S(1)}, u32[]{:S(2)}, u32[]{:S(2)}) collective-permute-start(bf16[2048,256]{1,0:T(8,128)(2,1)S(1)} %collective-permute-done.4.refs_0_), channel_id=1, source_target_pairs={{0,4},{4,8},{8,12},{1,5},{5,9},{9,13},{2,6},{6,10},{10,14},{3,7},{... | collective-permute-start | bytes 3145736 | tf_op jit(solution)/shard_map/ppermute | solution.py:371
  51.5 1.5 collective-permute-start.7
  53.0 0.6 collective-permute-start.11
  53.5 12.1 %rows.1.rows_ref = bf16[512,12544]{1,0:T(8,128)(2,1)S(1)} custom-call(s32[4]{0:T(128)S(1)} %pad_add_fusion.1.base_ref, s32[512,1]{1,0:T(8,128)S(1)} %copy.9.slots_ref, bf16[2048,256]{1,0:T(8,128)(2,1)S(1)} %bitcast.29, bf16[2048,256]{1,0:T(8,128)(2,1)} %collective-permute-done.1.refs_1_, bf16[2048,256]{1,0:T(8,128)(2,1)} %collective-permute-done.2.refs_2_, ...), custom_call_target="tpu_custom_call" | custom-call | tf_op jit(solution)/shard_map/rows/pallas_call | solution.py:192
  65.7 18.3 %correlate.4.refs_4_ = bf16[17,512,2048]{2,1,0:T(8,128)(2,1)} custom-call(s32[4]{0:T(128)S(1)} %pad_add_fusion.2.where_ref, bf16[512,12544]{1,0:T(8,128)(2,1)S(1)} %rows.1.rows_ref, s32[1,2048]{1,0:T(1,128)S(1)} %bitcast.31, bf16[2048,256]{1,0:T(8,128)(2,1)S(1)} %bitcast.30, bf16[2048,256]{1,0:T(8,128)(2,1)} %collective-permute-done.1.refs_1_), custom_call_target="tpu_custom_call" | custom-call | flops 18253611008 | bytes 23855104 | tf_op jit(solution)/shard_map/correlate/pallas_call | solution.py:308
  84.0 4.3 %collective-permute-start.12 = (bf16[2048,256]{1,0:T(8,128)(2,1)S(1)}, bf16[2048,256]{1,0:T(8,128)(2,1)S(1)}, u32[]{:S(2)}, u32[]{:S(2)}) collective-permute-start(bf16[2048,256]{1,0:T(8,128)(2,1)S(1)} %collective-permute-done.6.refs_2_.refs_0_), channel_id=1, source_target_pairs={{0,4},{4,8},{8,12},{1,5},{5,9},{9,13},{2,6},{6,10},{10,14},{3,7},{... | collective-permute-start | bytes 3145736 | tf_op jit(solution)/shard_map/ppermute | solution.py:371
  88.4 1.5 collective-permute-start.13
  89.9 0.5 collective-permute-start.9
  90.5 17.1 %correlate.5.refs_6_ = bf16[17,512,2048]{2,1,0:T(8,128)(2,1)} custom-call(s32[4]{0:T(128)S(1)} %pad_add_fusion.3.where_ref, bf16[512,12544]{1,0:T(8,128)(2,1)S(1)} %rows.1.rows_ref, s32[1,2048]{1,0:T(1,128)S(1)} %bitcast.32, bf16[2048,256]{1,0:T(8,128)(2,1)S(1)} %collective-permute-done.4.refs_0_, ...), custom_call_target="tpu_custom_call", output_to_operand_aliasing={{}: (7, {})} | custom-call | flops 18253611008 | bytes 23855104 | tf_op jit(solution)/shard_map/correlate/pallas_call | solution.py:308
  107.6 3.5 %collective-permute-done.12.refs_4_ = bf16[2048,256]{1,0:T(8,128)(2,1)S(1)} collective-permute-done((bf16[2048,256]{1,0:T(8,128)(2,1)S(1)}, bf16[2048,256]{1,0:T(8,128)(2,1)S(1)}, u32[]{:S(2)}, u32[]{:S(2)}) %collective-permute-start.12) | collective-permute-done | bytes 1048608 | tf_op jit(solution)/shard_map/ppermute | solution.py:371
  111.1 4.7 %collective-permute-done.13.refs_6_ = bf16[2048,256]{1,0:T(8,128)(2,1)S(1)} collective-permute-done((bf16[2048,256]{1,0:T(8,128)(2,1)S(1)}, bf16[2048,256]{1,0:T(8,128)(2,1)S(1)}, u32[]{:S(2)}, u32[]{:S(2)}) %collective-permute-start.13) | collective-permute-done | bytes 1048608 | tf_op jit(solution)/shard_map/ppermute | solution.py:371
  116.4 17.1 %correlate.6.refs_8_ = bf16[17,512,2048]{2,1,0:T(8,128)(2,1)} custom-call(s32[4]{0:T(128)S(1)} %pad_add_fusion.4.where_ref, bf16[512,12544]{1,0:T(8,128)(2,1)S(1)} %rows.1.rows_ref, s32[1,2048]{1,0:T(1,128)S(1)} %bitcast.33, bf16[2048,256]{1,0:T(8,128)(2,1)S(1)} %collective-permute-done.4.refs_0_, ...), custom_call_target="tpu_custom_call", output_to_operand_aliasing={{}: (9, {})} | custom-call | flops 18253611008 | bytes 23855104 | tf_op jit(solution)/shard_map/correlate/pallas_call | solution.py:308
  133.5 17.4 %correlate.7 = bf16[17,512,2048]{2,1,0:T(8,128)(2,1)} custom-call(s32[4]{0:T(128)S(1)} %pad_add_fusion.where_ref, bf16[512,12544]{1,0:T(8,128)(2,1)S(1)} %rows.1.rows_ref, s32[1,2048]{1,0:T(1,128)S(1)} %bitcast.34, bf16[2048,256]{1,0:T(8,128)(2,1)S(1)} %collective-permute-done.6.refs_2_.refs_0_, ...), custom_call_target="tpu_custom_call", output_to_operand_aliasing={{}: (11, {})} | custom-call | flops 18253611008 | bytes 23855104 | tf_op jit(solution)/shard_map/correlate/pallas_call | solution.py:308
  (31 shorter events, 2.8 us)
Async XLA Ops:
  0.0 41.9 %copy-start = (s32[1,1024]{1,0:T(1,128)S(1)}, s32[1,1024]{1,0:T(1,128)}, u32[]{:S(2)}) copy-start(s32[1,1024]{1,0:T(1,128)} %param.6) | copy-start | bytes 12292
  1.7 4.2 %collective-permute-start = (f32[2,1000,256]{2,1,0:T(8,128)S(1)}, f32[2,1000,256]{2,1,0:T(8,128)S(1)}, u32[]{:S(2)}, u32[]{:S(2)}) collective-permute-start(f32[2,1000,256]{2,1,0:T(8,128)S(1)} %dynamic-slice_bitcast_fusion), channel_id=1, source_target_pairs={{0,1},{1,0},{2,3},{3,2},{4,5},{5,4},{6,7},{7,6},{8,9},{9,8},{10,11... | collective-permute-start | bytes 6144008 | tf_op jit(solution)/shard_map/ppermute | solution.py:334
  6.0 2.2 %copy-start.2 = (f32[2,512,1000]{1,2,0:T(8,128)S(1)}, f32[2,512,1000]{1,2,0:T(8,128)}, u32[]{:S(2)}) copy-start(f32[2,512,1000]{1,2,0:T(8,128)} %param.4) | copy-start | bytes 12288004
  14.9 26.5 %collective-permute-start.2 = (bf16[2048,256]{1,0:T(8,128)(2,1)S(1)}, bf16[2048,256]{1,0:T(8,128)(2,1)}, u32[]{:S(2)}, u32[]{:S(2)}) collective-permute-start(bf16[2048,256]{1,0:T(8,128)(2,1)S(1)} %bitcast.25), channel_id=1, source_target_pairs={{0,2},{2,0},{1,3},{3,1},{4,6},{6,4},{5,7},{7,5},{8,10},{10,8},{9,1... | collective-permute-start | bytes 3145736 | tf_op jit(solution)/shard_map/ppermute | solution.py:334
  17.9 25.9 %collective-permute-start.4 = (bf16[2048,256]{1,0:T(8,128)(2,1)S(1)}, bf16[2048,256]{1,0:T(8,128)(2,1)S(1)}, u32[]{:S(2)}, u32[]{:S(2)}) collective-permute-start(bf16[2048,256]{1,0:T(8,128)(2,1)S(1)} %bitcast.26), channel_id=1, source_target_pairs={{0,4},{4,8},{8,12},{1,5},{5,9},{9,13},{2,6},{6,10},{10,14},{3,7},{... | collective-permute-start | bytes 3145736 | tf_op jit(solution)/shard_map/ppermute | solution.py:371
  21.4 26.5 %collective-permute-start.5 = (bf16[2048,256]{1,0:T(8,128)(2,1)S(1)}, bf16[2048,256]{1,0:T(8,128)(2,1)S(1)}, u32[]{:S(2)}, u32[]{:S(2)}) collective-permute-start(bf16[2048,256]{1,0:T(8,128)(2,1)S(1)} %bitcast.27), channel_id=1, source_target_pairs={{4,0},{8,4},{12,8},{5,1},{9,5},{13,9},{6,2},{10,6},{14,10},{7,3},{... | collective-permute-start | bytes 3145736 | tf_op jit(solution)/shard_map/ppermute | solution.py:371
  41.4 6.5 %collective-permute-start.3 = (bf16[2048,256]{1,0:T(8,128)(2,1)}, bf16[2048,256]{1,0:T(8,128)(2,1)}, u32[]{:S(2)}, u32[]{:S(2)}) collective-permute-start(bf16[2048,256]{1,0:T(8,128)(2,1)} %collective-permute-done.2.refs_2_), channel_id=1, source_target_pairs={{0,1},{1,0},{2,3},{3,2},{4,5},{5,4},{6,7},{7,6},{8,9},{9,8},{10,11... | collective-permute-start | bytes 3145736 | tf_op jit(solution)/shard_map/ppermute | solution.py:334
  41.4 12.1 %collective-permute-start.1 = (bf16[2048,256]{1,0:T(8,128)(2,1)S(1)}, bf16[2048,256]{1,0:T(8,128)(2,1)}, u32[]{:S(2)}, u32[]{:S(2)}) collective-permute-start(bf16[2048,256]{1,0:T(8,128)(2,1)S(1)} %bitcast.28), channel_id=1, source_target_pairs={{0,1},{1,0},{2,3},{3,2},{4,5},{5,4},{6,7},{7,6},{8,9},{9,8},{10,11... | collective-permute-start | bytes 3145736 | tf_op jit(solution)/shard_map/ppermute | solution.py:334
  47.9 36.0 %collective-permute-start.6 = (bf16[2048,256]{1,0:T(8,128)(2,1)S(1)}, bf16[2048,256]{1,0:T(8,128)(2,1)S(1)}, u32[]{:S(2)}, u32[]{:S(2)}) collective-permute-start(bf16[2048,256]{1,0:T(8,128)(2,1)S(1)} %collective-permute-done.4.refs_0_), channel_id=1, source_target_pairs={{0,4},{4,8},{8,12},{1,5},{5,9},{9,13},{2,6},{6,10},{10,14},{3,7},{... | collective-permute-start | bytes 3145736 | tf_op jit(solution)/shard_map/ppermute | solution.py:371
  51.4 38.5 %collective-permute-start.10 = (bf16[2048,256]{1,0:T(8,128)(2,1)S(1)}, bf16[2048,256]{1,0:T(8,128)(2,1)S(1)}, u32[]{:S(2)}, u32[]{:S(2)}) collective-permute-start(bf16[2048,256]{1,0:T(8,128)(2,1)S(1)} %collective-permute-done.4.refs_0_), channel_id=1, source_target_pairs={{0,1},{1,0},{2,3},{3,2},{4,5},{5,4},{6,7},{7,6},{8,9},{9,8},{10,11... | collective-permute-start | bytes 3145736 | tf_op jit(solution)/shard_map/ppermute | solution.py:334
  51.5 32.5 %collective-permute-start.7 = (bf16[2048,256]{1,0:T(8,128)(2,1)S(1)}, bf16[2048,256]{1,0:T(8,128)(2,1)S(1)}, u32[]{:S(2)}, u32[]{:S(2)}) collective-permute-start(bf16[2048,256]{1,0:T(8,128)(2,1)S(1)} %collective-permute-done.5.refs_2_), channel_id=1, source_target_pairs={{4,0},{8,4},{12,8},{5,1},{9,5},{13,9},{6,2},{10,6},{14,10},{7,3},{... | collective-permute-start | bytes 3145736 | tf_op jit(solution)/shard_map/ppermute | solution.py:371
  53.0 37.5 %collective-permute-start.11 = (bf16[2048,256]{1,0:T(8,128)(2,1)S(1)}, bf16[2048,256]{1,0:T(8,128)(2,1)S(1)}, u32[]{:S(2)}, u32[]{:S(2)}) collective-permute-start(bf16[2048,256]{1,0:T(8,128)(2,1)S(1)} %collective-permute-done.5.refs_2_), channel_id=1, source_target_pairs={{0,1},{1,0},{2,3},{3,2},{4,5},{5,4},{6,7},{7,6},{8,9},{9,8},{10,11... | collective-permute-start | bytes 3145736 | tf_op jit(solution)/shard_map/ppermute | solution.py:334
  84.0 27.2 %collective-permute-start.12 = (bf16[2048,256]{1,0:T(8,128)(2,1)S(1)}, bf16[2048,256]{1,0:T(8,128)(2,1)S(1)}, u32[]{:S(2)}, u32[]{:S(2)}) collective-permute-start(bf16[2048,256]{1,0:T(8,128)(2,1)S(1)} %collective-permute-done.6.refs_2_.refs_0_), channel_id=1, source_target_pairs={{0,4},{4,8},{8,12},{1,5},{5,9},{9,13},{2,6},{6,10},{10,14},{3,7},{... | collective-permute-start | bytes 3145736 | tf_op jit(solution)/shard_map/ppermute | solution.py:371
  88.3 28.0 %collective-permute-start.8 = (bf16[2048,256]{1,0:T(8,128)(2,1)S(1)}, bf16[2048,256]{1,0:T(8,128)(2,1)S(1)}, u32[]{:S(2)}, u32[]{:S(2)}) collective-permute-start(bf16[2048,256]{1,0:T(8,128)(2,1)S(1)} %collective-permute-done.6.refs_2_.refs_0_), channel_id=1, source_target_pairs={{0,1},{1,0},{2,3},{3,2},{4,5},{5,4},{6,7},{7,6},{8,9},{9,8},{10,11... | collective-permute-start | bytes 3145736 | tf_op jit(solution)/shard_map/ppermute | solution.py:334
  88.4 27.4 %collective-permute-start.13 = (bf16[2048,256]{1,0:T(8,128)(2,1)S(1)}, bf16[2048,256]{1,0:T(8,128)(2,1)S(1)}, u32[]{:S(2)}, u32[]{:S(2)}) collective-permute-start(bf16[2048,256]{1,0:T(8,128)(2,1)S(1)} %collective-permute-done.7.refs_4_.refs_2_), channel_id=1, source_target_pairs={{4,0},{8,4},{12,8},{5,1},{9,5},{13,9},{6,2},{10,6},{14,10},{7,3},{... | collective-permute-start | bytes 3145736 | tf_op jit(solution)/shard_map/ppermute | solution.py:371
  89.9 26.4 %collective-permute-start.9 = (bf16[2048,256]{1,0:T(8,128)(2,1)S(1)}, bf16[2048,256]{1,0:T(8,128)(2,1)S(1)}, u32[]{:S(2)}, u32[]{:S(2)}) collective-permute-start(bf16[2048,256]{1,0:T(8,128)(2,1)S(1)} %collective-permute-done.7.refs_4_.refs_2_), channel_id=1, source_target_pairs={{0,1},{1,0},{2,3},{3,2},{4,5},{5,4},{6,7},{7,6},{8,9},{9,8},{10,11... | collective-permute-start | bytes 3145736 | tf_op jit(solution)/shard_map/ppermute | solution.py:334
  115.8 17.7 %collective-permute-start.14 = (bf16[2048,256]{1,0:T(8,128)(2,1)S(1)}, bf16[2048,256]{1,0:T(8,128)(2,1)S(1)}, u32[]{:S(2)}, u32[]{:S(2)}) collective-permute-start(bf16[2048,256]{1,0:T(8,128)(2,1)S(1)} %collective-permute-done.12.refs_4_), channel_id=1, source_target_pairs={{0,1},{1,0},{2,3},{3,2},{4,5},{5,4},{6,7},{7,6},{8,9},{9,8},{10,11... | collective-permute-start | bytes 3145736 | tf_op jit(solution)/shard_map/ppermute | solution.py:334
  115.8 17.7 %collective-permute-start.15 = (bf16[2048,256]{1,0:T(8,128)(2,1)S(1)}, bf16[2048,256]{1,0:T(8,128)(2,1)S(1)}, u32[]{:S(2)}, u32[]{:S(2)}) collective-permute-start(bf16[2048,256]{1,0:T(8,128)(2,1)S(1)} %collective-permute-done.13.refs_6_), channel_id=1, source_target_pairs={{0,1},{1,0},{2,3},{3,2},{4,5},{5,4},{6,7},{7,6},{8,9},{9,8},{10,11... | collective-permute-start | bytes 3145736 | tf_op jit(solution)/shard_map/ppermute | solution.py:334
  133.5 17.4 %copy-start.1 = (s32[1,1024]{1,0:T(1,128)S(1)}, s32[1,1024]{1,0:T(1,128)}, u32[]{:S(2)}) copy-start(s32[1,1024]{1,0:T(1,128)} %param.6) | copy-start | bytes 12292
